TPU v7x, 256 devices: a whole 4x4x8 slice. The times are simulated.
256 devices in a mesh: row: 32 (over x_hi, z, core), feat: 8 (over y, x_lo).
Axes of the slice: x: 4 (x_hi: 2, x_lo: 2; x = x_hi * 2 + x_lo), y: 4, z: 8, core: 2. Of those that a mesh axis runs over, the one named last changes fastest.
Arguments:
- bin_index: int32 [1024, 98304], P('feat', 'row'), may hold values from 0 to 63
- gradient: bfloat16 [32, 98304], P(None, ('row', 'feat')), may hold values from -6 to 6
- hessian: bfloat16 [98304], P(('row', 'feat')), may hold values from 0.25 to 4
- row_node: int32 [98304], P('row'), may hold values from 0 to 7
Outputs:
- split_gain: float32 [1024, 512], P(('feat', 'row'))
- best_gain: float32 [8], replicated
All inputs are finite; a program needn't handle non-finite values.
Results may differ from a plain program's by a relative error of at most 0.0003.
Values may be sent and summed in bfloat16 or wider, within the bound.
No kernel may reach another device: no remote copies, remote signals or barrier semaphores. Data moves between devices by JAX's collectives and lax.ppermute only.
A program may use at most 128 MiB of HBM per device.

v0:
```python
import functools
import math
import jax
import jax.numpy as jnp
from jax import lax
from jax.sharding import Mesh
from jax.sharding import PartitionSpec as P

BINS = 64
NODES = 8
ROW = ("row_0", "row_1", "row_2")
FEAT = ("feat_0", "feat_1")
ROW_FEAT = ("row_0", "row_1", "row_2", "feat_0", "feat_1")
FEAT_ROW = ("feat_0", "feat_1", "row_0", "row_1", "row_2")
ridge_term = 1.0


def by_axis(x, axes):
    return functools.reduce(lax.psum, axes, x)


def gather_turned(arrays, axis, dims):
    turned = [jnp.moveaxis(a, dim, 0) for a, dim in zip(arrays, dims)]
    both = jnp.concatenate([t.reshape(len(t), -1) for t in turned], axis=1)
    result, at, gathered = (lax.all_gather(both, axis, axis=0, tiled=True), 0, [])
    for t, dim in zip(turned, dims):
        section = result[:, at : at + t[0].size].reshape(-1, *t.shape[1:])
        gathered.append(jnp.moveaxis(section, 0, dim))
        at += t[0].size
    return tuple(gathered)


def one_axis_at_a_time(x, axes):
    for axis in axes:
        x = lax.pmax(x, axis)
    return x


def masked_rows(node_ids, grad_rows, hess_rows):
    stacked = jnp.concatenate([grad_rows, hess_rows[None, :]], 0)
    picked = (node_ids[None, :] == jnp.arange(NODES, dtype=jnp.int32)[:, None]).astype(jnp.bfloat16)
    return (picked[:, None, :] * stacked[None, :, :]).reshape(-1, node_ids.shape[0])


def histogram_block(feature_block, masked):
    levels = jnp.arange(BINS, dtype=jnp.int32)
    onehot = (feature_block[:, None, :] == levels[None, :, None]).astype(jnp.bfloat16)
    return jnp.einsum("fbr,mr->fbm", onehot, masked, preferred_element_type=jnp.float32)


def score_splits(histogram, node_totals):
    left_sums = jnp.cumsum(histogram, axis=1)
    whole_sums = node_totals[None, None]
    right_sums = whole_sums - left_sums

    def part_score(sums):
        return jnp.sum(sums[..., :-1] * sums[..., :-1], axis=-1) / (sums[..., -1] + ridge_term)

    outputs_count = histogram.shape[-1] - 1
    score_terms = part_score(left_sums) + part_score(right_sums) - part_score(whole_sums)
    return jnp.transpose(0.5 / outputs_count * score_terms, (0, 2, 1))


def on_device(bin_index, gradient, hessian, row_node):
    local_features = bin_index.shape[0]
    owned_count = local_features // lax.axis_size(ROW)
    outputs_count = gradient.shape[0]
    shard_rows = gradient.shape[1]
    first_local = lax.axis_index(FEAT) * shard_rows
    local_nodes = lax.dynamic_slice_in_dim(row_node, first_local, shard_rows, 0)
    stacked = jnp.concatenate([gradient, hessian[None, :]], 0)
    picked = (local_nodes[None, :] == jnp.arange(NODES, dtype=jnp.int32)[:, None]).astype(
        jnp.bfloat16
    )
    local_totals = jnp.einsum("nr,mr->nm", picked, stacked, preferred_element_type=jnp.float32)
    node_totals = by_axis(local_totals, ROW_FEAT)
    grad_rows, hess_rows = gather_turned((gradient, hessian), FEAT, (1, 0))
    masked = masked_rows(row_node, grad_rows, hess_rows)
    group_size = math.gcd(owned_count * lax.axis_size(ROW), 16)

    def one_group(step_index):
        feature_block = lax.dynamic_slice_in_dim(bin_index, step_index * group_size, group_size, 0)
        return histogram_block(feature_block, masked).reshape(group_size, -1)

    pieces = lax.map(
        one_group, jnp.arange(owned_count * lax.axis_size(ROW) // group_size, dtype=jnp.int32)
    )
    owned = lax.psum_scatter(
        pieces.reshape(owned_count * lax.axis_size(ROW), -1), ROW, scatter_dimension=0, tiled=True
    )
    histogram = owned.reshape(owned_count, BINS, NODES, outputs_count + 1)
    split_gain = score_splits(histogram, node_totals)
    best_gain = one_axis_at_a_time(jnp.max(split_gain, axis=(0, 2)), ROW_FEAT)
    return (split_gain.reshape(owned_count, NODES * BINS), best_gain)


def solution(mesh):
    split = Mesh(
        mesh.devices.reshape(2, 8, 2, 4, 2), ("row_0", "row_1", "row_2", "feat_0", "feat_1")
    )
    in_specs = (P(FEAT, ROW), P(None, ROW_FEAT), P(ROW_FEAT), P(ROW))
    out_specs = (P(FEAT_ROW, None), P())
    return jax.shard_map(
        on_device, mesh=split, in_specs=in_specs, out_specs=out_specs, check_vma=False
    )
```

profile of v0, /device:TPU:32, one launch (start us, length us, event | category | flops | bytes accessed | tf_op | source)
XLA Modules:
  0.0 494.6 jit_solution(4943222124883276265)
XLA Ops:
  8.6 29.1 %all_gather.3 = bf16[3072,33]{0,1:T(8,128)(2,1)S(1)} all-gather(bf16[384,33]{0,1:T(8,128)(2,1)S(1)} %pad_maximum_fusion.1), channel_id=1, replica_groups=mesh['row_0'=2,'row_1'=8,'row_2'=2,'feat_0'=4,'feat_1'=2] {'feat_0','fea..., dimensions={0}, use_global_device_ids=true | all-gather | bytes 228096 | tf_op jit(solution)/shard_map/all_gather | solution.py:25
  38.5 86.3 %while.11 = (s32[]{:T(128)}, f32[8,16,16896]{2,1,0:T(8,128)}, s32[8]{0:T(128)S(1)}, s32[128,3072]{1,0:T(8,128)}, bf16[33,3072]{1,0:T(8,128)(2,1)S(1)}, /*index=5...) while((s32[]{:T(128)}, f32[8,16,16896]{2,1,0:T(8,128)}, ...), condition=%wide.region_1.0_spmd.clone, body=%wide.region_0.0_spmd.clone.sunk | while | flops 1664901120 | bytes 12736687 | solution.py:85
  38.7 1.7 reshape.73
  42.6 4.8 fusion.28
  49.5 1.7 reshape.73
  53.4 4.8 fusion.28
  64.2 4.8 fusion.28
  75.0 4.8 fusion.28
  85.8 4.8 fusion.28
  96.6 4.8 fusion.28
  107.3 4.8 fusion.28
  118.1 4.8 fusion.28
  126.4 6.4 %psum.35 = f32[8,33]{1,0:T(8,128)S(1)} all-reduce(f32[8,33]{1,0:T(8,128)S(1)} %fusion.7), channel_id=1, replica_groups=mesh['row_0'=2,'row_1'=8,'row_2'=2,'feat_0'=4,'feat_1'=2] {'row_0'}, use_global_device_ids=true, to_apply=%region_5.6 | all-reduce | flops 264 | bytes 2112 | tf_op jit(solution)/shard_map/psum | solution.py:19
  132.8 17.9 %psum.36 = f32[8,33]{1,0:T(8,128)S(1)} all-reduce(f32[8,33]{1,0:T(8,128)S(1)} %psum.35), channel_id=1, replica_groups=mesh['row_0'=2,'row_1'=8,'row_2'=2,'feat_0'=4,'feat_1'=2] {'row_1'}, use_global_device_ids=true, to_apply=%region_6.7 | all-reduce | flops 264 | bytes 2112 | tf_op jit(solution)/shard_map/psum | solution.py:19
  150.7 2.5 psum.37
  153.2 8.3 %psum.38 = f32[8,33]{1,0:T(8,128)S(1)} all-reduce(f32[8,33]{1,0:T(8,128)S(1)} %psum.37), channel_id=1, replica_groups=mesh['row_0'=2,'row_1'=8,'row_2'=2,'feat_0'=4,'feat_1'=2] {'feat_0'}, use_global_device_ids=true, to_apply=%region_8.9 | all-reduce | flops 264 | bytes 2112 | tf_op jit(solution)/shard_map/psum | solution.py:19
  161.5 6.6 %psum.39 = f32[8,33]{1,0:T(8,128)S(1)} all-reduce(f32[8,33]{1,0:T(8,128)S(1)} %psum.38), channel_id=1, replica_groups=mesh['row_0'=2,'row_1'=8,'row_2'=2,'feat_0'=4,'feat_1'=2] {'feat_1'}, use_global_device_ids=true, to_apply=%region_9.10 | all-reduce | flops 264 | bytes 2112 | tf_op jit(solution)/shard_map/psum | solution.py:19
  169.7 243.3 %all-reduce.3.cloned.1.call-done = f32[128,16896]{1,0:T(8,128)} async-done(((f32[128,16896]{1,0:T(8,128)}), f32[128,16896]{1,0:T(8,128)}) %all-reduce.3.cloned.1.call-update) | async-done | bytes 8650768
  415.3 25.9 %fusion.22 = f32[4,64,8,33]{3,2,1,0:T(8,128)S(1)} fusion(f32[4,64,8,33]{3,2,1,0:T(8,128)S(1)} %reshape.66), kind=kOutput, calls=%fused_computation.38 | output fusion | flops 4257792 | bytes 540672 | tf_op jit(solution)/shard_map/jit(cumsum)/reduce_window_sum | solution.py:52
  442.4 6.4 %pmax.35 = f32[8]{0:T(128)S(1)} all-reduce(f32[8]{0:T(128)S(1)} %get-tuple-element.58), channel_id=1, replica_groups=mesh['row_0'=2,'row_1'=8,'row_2'=2,'feat_0'=4,'feat_1'=2] {'row_0'}, use_global_device_ids=true, to_apply=%region_13.14 | all-reduce | flops 8 | bytes 64 | tf_op jit(solution)/shard_map/pmax | solution.py:35
  448.8 19.9 %pmax.36 = f32[8]{0:T(128)S(1)} all-reduce(f32[8]{0:T(128)S(1)} %pmax.35), channel_id=1, replica_groups=mesh['row_0'=2,'row_1'=8,'row_2'=2,'feat_0'=4,'feat_1'=2] {'row_1'}, use_global_device_ids=true, to_apply=%region_14.15 | all-reduce | flops 8 | bytes 64 | tf_op jit(solution)/shard_map/pmax | solution.py:35
  468.8 2.5 pmax.37
  471.2 10.4 %pmax.38 = f32[8]{0:T(128)S(1)} all-reduce(f32[8]{0:T(128)S(1)} %pmax.37), channel_id=1, replica_groups=mesh['row_0'=2,'row_1'=8,'row_2'=2,'feat_0'=4,'feat_1'=2] {'feat_0'}, use_global_device_ids=true, to_apply=%region_16.17 | all-reduce | flops 8 | bytes 64 | tf_op jit(solution)/shard_map/pmax | solution.py:35
  482.4 5.4 %pmax.39 = f32[8]{0:T(128)} all-reduce(f32[8]{0:T(128)S(1)} %pmax.38), channel_id=1, replica_groups=mesh['row_0'=2,'row_1'=8,'row_2'=2,'feat_0'=4,'feat_1'=2] {'feat_1'}, use_global_device_ids=true, to_apply=%region_17.18 | all-reduce | flops 8 | bytes 64 | tf_op jit(solution)/shard_map/pmax | solution.py:35
  (79 shorter events, 47.6 us)
Async XLA Ops:
  7.2 405.9 %all-reduce.3.cloned.1.call-start = ((), (), s32[]{:S(2)}) async-start(), calls=%async_computation | async-start | bytes 17301504
  124.8 0.7 copy-start.1
  124.8 1.5 copy-start
  124.8 43.7 %copy-start.2 = (u32[256]{0:T(256)S(1)}, u32[256]{0:T(256)}, u32[]{:S(2)}) copy-start(u32[256]{0:T(256)} %constant.46) | copy-start | bytes 3076
Sparse Core Ops, SparseCore 0:
  125.0 287.9 all-reduce.2
where the time goes:
time: 496 us; the launch traced here: 495 us
  waiting for transfers between devices  243 us (49%)
  blocking collectives  115 us (23%)
  local copies, waits for them, and re-layouts  47.1 us (9%)
  matrix products  38.9 us (8%)
  other arithmetic  29.7 us (6%)
  between operations  14.8 us (3%)
  loops' own time  5.37 us (1%)
    unnamed x2, waiting for transfers between devices  243 us
    pmax x5, blocking collectives, one_axis_at_a_time(): x = lax.pmax(x, axis)  44.7 us
    psum x5, blocking collectives, by_axis(): return functools.reduce(lax.psum, axes, x)  41.7 us
    dot_general x8, matrix products, histogram_block(): jnp.einsum('fbr,mr->fbm', onehot, masked, preferred_element_type=jnp.floa...  38.8 us
    all_gather x1, blocking collectives, gather_turned(): lax.all_gather(both, axis, axis=0, tiled=True)  29.1 us
    another operation x1, other arithmetic, score_splits(): left_sums = jnp.cumsum(histogram, axis=1)  25.9 us
    mul x8, local copies, waits for them, and re-layouts, masked_rows(): picked[:, None, :] * stacked[None, :, :]  13.8 us
  transfers between devices with their start and end apart: 1, of which 1 were waited for; matrix products, arithmetic and copies ran while one was open for 0% of the time, Pallas kernels for 0%

commit v1 on v0

--- a/solution.py
+++ b/solution.py
@@ -22,7 +22,13 @@
 def gather_turned(arrays, axis, dims):
     turned = [jnp.moveaxis(a, dim, 0) for a, dim in zip(arrays, dims)]
     both = jnp.concatenate([t.reshape(len(t), -1) for t in turned], axis=1)
-    result, at, gathered = (lax.all_gather(both, axis, axis=0, tiled=True), 0, [])
+    result, at, gathered = (
+        jnp.concatenate(
+            lax.all_to_all(jnp.stack([both] * lax.axis_size(axis)), axis, 0, 0), axis=0
+        ),
+        0,
+        [],
+    )
     for t, dim in zip(turned, dims):
         section = result[:, at : at + t[0].size].reshape(-1, *t.shape[1:])
         gathered.append(jnp.moveaxis(section, 0, dim))

time: 496 us -> 478 us (0.964)
  blocking collectives: 115 us -> 85 us
  waiting for transfers between devices: 243 us -> 250 us
  starting transfers between devices: 0.04 us -> 5.43 us
    all_gather x1 -> x0, blocking collectives: 29.1 us -> none  [gather_turned(): lax.all_gather(both, axis, axis=0, tiled=True)]
    all_to_all x0 -> x1, waiting for transfers between devices: none -> 6.42 us  [gather_turned(): lax.all_to_all(jnp.stack([both] * lax.axis_size(axis)), axis, 0, 0)]
    all_to_all x0 -> x1, starting transfers between devices: none -> 5.4 us  [gather_turned(): lax.all_to_all(jnp.stack([both] * lax.axis_size(axis)), axis, 0, 0)]
  transfers between devices with their start and end apart: 1 -> 2, of which waited for: 1 -> 2; matrix products, arithmetic and copies ran while one was open for 0% -> 1% of each run, Pallas kernels for 0% -> 0%
where the time goes in v1:
time: 478 us; the launch traced here: 477 us
  waiting for transfers between devices  250 us (52%)
  blocking collectives  85 us (18%)
  local copies, waits for them, and re-layouts  48.1 us (10%)
  matrix products  38.9 us (8%)
  other arithmetic  29.7 us (6%)
  between operations  14.8 us (3%)
  starting transfers between devices  5.43 us (1%)
  loops' own time  5.37 us (1%)
    unnamed x2, waiting for transfers between devices  243 us
    pmax x5, blocking collectives, one_axis_at_a_time(): x = lax.pmax(x, axis)  44.7 us
    psum x5, blocking collectives, by_axis(): return functools.reduce(lax.psum, axes, x)  40.3 us
    dot_general x8, matrix products, histogram_block(): jnp.einsum('fbr,mr->fbm', onehot, masked, preferred_element_type=jnp.floa...  38.8 us
    another operation x1, other arithmetic, score_splits(): left_sums = jnp.cumsum(histogram, axis=1)  25.9 us
    mul x8, local copies, waits for them, and re-layouts, masked_rows(): picked[:, None, :] * stacked[None, :, :]  14.1 us
  transfers between devices with their start and end apart: 2, of which 2 were waited for; matrix products, arithmetic and copies ran while one was open for 1% of the time, Pallas kernels for 0%

profile of v1, /device:TPU:32, one launch (start us, length us, event | category | flops | bytes accessed | tf_op | source)
XLA Modules:
  0.0 477.0 jit_solution(6063569724686855559)
XLA Ops:
  9.3 5.4 %all-to-all-start = ((bf16[8,384,33]{1,2,0:T(8,128)(2,1)}), bf16[8,384,33]{1,2,0:T(8,128)(2,1)S(1)}, u32[]{:S(2)}, u32[]{:S(2)}) async-start(bf16[8,384,33]{1,2,0:T(8,128)(2,1)} %stack.2), calls=%async_computation | async-start | bytes 491520 | tf_op jit(solution)/shard_map/all_to_all | solution.py:27
  15.5 6.4 %all-to-all-done = bf16[8,384,33]{1,2,0:T(8,128)(2,1)S(1)} async-done(((bf16[8,384,33]{1,2,0:T(8,128)(2,1)}), bf16[8,384,33]{1,2,0:T(8,128)(2,1)S(1)}, u32[]{:S(2)}, u32[]{:S(2)}) %all-to-all-start) | async-done | bytes 202784 | tf_op jit(solution)/shard_map/all_to_all | solution.py:27
  22.1 86.5 %while.11 = (s32[]{:T(128)}, f32[8,16,16896]{2,1,0:T(8,128)}, s32[8]{0:T(128)S(1)}, s32[128,3072]{1,0:T(8,128)}, bf16[33,3072]{1,0:T(8,128)(2,1)S(1)}, /*index=5...) while((s32[]{:T(128)}, f32[8,16,16896]{2,1,0:T(8,128)}, ...), condition=%wide.region_1.0_spmd.clone, body=%wide.region_0.0_spmd.clone.sunk | while | flops 1664901120 | bytes 12736687 | solution.py:91
  22.3 1.8 reshape.79
  26.2 4.8 %fusion.28 = f32[16,64,264]{2,1,0:T(8,128)S(1)} fusion(bf16[264,3072,1]{1,0,2:T(8,128)(2,1)} %reshape.79, s32[16,3072]{1,0:T(8,128)S(1)} %constant_dynamic-slice_fusion.3), kind=kOutput, calls=%fused_computation.2.clone.1 | convolution fusion | flops 1664090112 | bytes 2899968 | tf_op jit(solution)/shard_map/while/body/eval_jaxpr/fbr,mr->fbm/dot_general | solution.py:54
  37.0 4.8 %fusion.28 = f32[16,64,264]{2,1,0:T(8,128)S(1)} fusion(bf16[264,3072,1]{1,0,2:T(8,128)(2,1)} %reshape.79, s32[16,3072]{1,0:T(8,128)S(1)} %constant_dynamic-slice_fusion.3), kind=kOutput, calls=%fused_computation.2.clone.1 | convolution fusion | flops 1664090112 | bytes 2899968 | tf_op jit(solution)/shard_map/while/body/eval_jaxpr/fbr,mr->fbm/dot_general | solution.py:54
  47.9 4.8 %fusion.28 = f32[16,64,264]{2,1,0:T(8,128)S(1)} fusion(bf16[264,3072,1]{1,0,2:T(8,128)(2,1)} %reshape.79, s32[16,3072]{1,0:T(8,128)S(1)} %constant_dynamic-slice_fusion.3), kind=kOutput, calls=%fused_computation.2.clone.1 | convolution fusion | flops 1664090112 | bytes 2899968 | tf_op jit(solution)/shard_map/while/body/eval_jaxpr/fbr,mr->fbm/dot_general | solution.py:54
  58.7 4.8 %fusion.28 = f32[16,64,264]{2,1,0:T(8,128)S(1)} fusion(bf16[264,3072,1]{1,0,2:T(8,128)(2,1)} %reshape.79, s32[16,3072]{1,0:T(8,128)S(1)} %constant_dynamic-slice_fusion.3), kind=kOutput, calls=%fused_computation.2.clone.1 | convolution fusion | flops 1664090112 | bytes 2899968 | tf_op jit(solution)/shard_map/while/body/eval_jaxpr/fbr,mr->fbm/dot_general | solution.py:54
  69.5 4.8 %fusion.28 = f32[16,64,264]{2,1,0:T(8,128)S(1)} fusion(bf16[264,3072,1]{1,0,2:T(8,128)(2,1)} %reshape.79, s32[16,3072]{1,0:T(8,128)S(1)} %constant_dynamic-slice_fusion.3), kind=kOutput, calls=%fused_computation.2.clone.1 | convolution fusion | flops 1664090112 | bytes 2899968 | tf_op jit(solution)/shard_map/while/body/eval_jaxpr/fbr,mr->fbm/dot_general | solution.py:54
  80.3 4.8 %fusion.28 = f32[16,64,264]{2,1,0:T(8,128)S(1)} fusion(bf16[264,3072,1]{1,0,2:T(8,128)(2,1)} %reshape.79, s32[16,3072]{1,0:T(8,128)S(1)} %constant_dynamic-slice_fusion.3), kind=kOutput, calls=%fused_computation.2.clone.1 | convolution fusion | flops 1664090112 | bytes 2899968 | tf_op jit(solution)/shard_map/while/body/eval_jaxpr/fbr,mr->fbm/dot_general | solution.py:54
  91.1 4.8 %fusion.28 = f32[16,64,264]{2,1,0:T(8,128)S(1)} fusion(bf16[264,3072,1]{1,0,2:T(8,128)(2,1)} %reshape.79, s32[16,3072]{1,0:T(8,128)S(1)} %constant_dynamic-slice_fusion.3), kind=kOutput, calls=%fused_computation.2.clone.1 | convolution fusion | flops 1664090112 | bytes 2899968 | tf_op jit(solution)/shard_map/while/body/eval_jaxpr/fbr,mr->fbm/dot_general | solution.py:54
  101.9 4.8 %fusion.28 = f32[16,64,264]{2,1,0:T(8,128)S(1)} fusion(bf16[264,3072,1]{1,0,2:T(8,128)(2,1)} %reshape.79, s32[16,3072]{1,0:T(8,128)S(1)} %constant_dynamic-slice_fusion.3), kind=kOutput, calls=%fused_computation.2.clone.1 | convolution fusion | flops 1664090112 | bytes 2899968 | tf_op jit(solution)/shard_map/while/body/eval_jaxpr/fbr,mr->fbm/dot_general | solution.py:54
  110.2 6.4 %psum.35 = f32[8,33]{1,0:T(8,128)S(1)} all-reduce(f32[8,33]{1,0:T(8,128)S(1)} %fusion.7), channel_id=1, replica_groups=mesh['row_0'=2,'row_1'=8,'row_2'=2,'feat_0'=4,'feat_1'=2] {'row_0'}, use_global_device_ids=true, to_apply=%region_5.6 | all-reduce | flops 264 | bytes 2112 | tf_op jit(solution)/shard_map/psum | solution.py:19
  116.6 17.9 %psum.36 = f32[8,33]{1,0:T(8,128)S(1)} all-reduce(f32[8,33]{1,0:T(8,128)S(1)} %psum.35), channel_id=1, replica_groups=mesh['row_0'=2,'row_1'=8,'row_2'=2,'feat_0'=4,'feat_1'=2] {'row_1'}, use_global_device_ids=true, to_apply=%region_6.7 | all-reduce | flops 264 | bytes 2112 | tf_op jit(solution)/shard_map/psum | solution.py:19
  134.5 2.5 psum.37
  137.0 8.6 %psum.38 = f32[8,33]{1,0:T(8,128)S(1)} all-reduce(f32[8,33]{1,0:T(8,128)S(1)} %psum.37), channel_id=1, replica_groups=mesh['row_0'=2,'row_1'=8,'row_2'=2,'feat_0'=4,'feat_1'=2] {'feat_0'}, use_global_device_ids=true, to_apply=%region_8.9 | all-reduce | flops 264 | bytes 2112 | tf_op jit(solution)/shard_map/psum | solution.py:19
  145.5 4.9 %psum.39 = f32[8,33]{1,0:T(8,128)S(1)} all-reduce(f32[8,33]{1,0:T(8,128)S(1)} %psum.38), channel_id=1, replica_groups=mesh['row_0'=2,'row_1'=8,'row_2'=2,'feat_0'=4,'feat_1'=2] {'feat_1'}, use_global_device_ids=true, to_apply=%region_9.10 | all-reduce | flops 264 | bytes 2112 | tf_op jit(solution)/shard_map/psum | solution.py:19
  152.1 243.2 %all-reduce.3.cloned.1.call-done = f32[128,16896]{1,0:T(8,128)} async-done(((f32[128,16896]{1,0:T(8,128)}), f32[128,16896]{1,0:T(8,128)}) %all-reduce.3.cloned.1.call-update) | async-done | bytes 8650768
  397.6 25.9 %fusion.22 = f32[4,64,8,33]{3,2,1,0:T(8,128)S(1)} fusion(f32[4,64,8,33]{3,2,1,0:T(8,128)S(1)} %reshape.72), kind=kOutput, calls=%fused_computation.39 | output fusion | flops 4257792 | bytes 540672 | tf_op jit(solution)/shard_map/jit(cumsum)/reduce_window_sum | solution.py:58
  424.7 6.4 %pmax.35 = f32[8]{0:T(128)S(1)} all-reduce(f32[8]{0:T(128)S(1)} %get-tuple-element.58), channel_id=1, replica_groups=mesh['row_0'=2,'row_1'=8,'row_2'=2,'feat_0'=4,'feat_1'=2] {'row_0'}, use_global_device_ids=true, to_apply=%region_13.14 | all-reduce | flops 8 | bytes 64 | tf_op jit(solution)/shard_map/pmax | solution.py:41
  431.2 19.9 %pmax.36 = f32[8]{0:T(128)S(1)} all-reduce(f32[8]{0:T(128)S(1)} %pmax.35), channel_id=1, replica_groups=mesh['row_0'=2,'row_1'=8,'row_2'=2,'feat_0'=4,'feat_1'=2] {'row_1'}, use_global_device_ids=true, to_apply=%region_14.15 | all-reduce | flops 8 | bytes 64 | tf_op jit(solution)/shard_map/pmax | solution.py:41
  451.1 2.5 pmax.37
  453.6 10.4 %pmax.38 = f32[8]{0:T(128)S(1)} all-reduce(f32[8]{0:T(128)S(1)} %pmax.37), channel_id=1, replica_groups=mesh['row_0'=2,'row_1'=8,'row_2'=2,'feat_0'=4,'feat_1'=2] {'feat_0'}, use_global_device_ids=true, to_apply=%region_16.17 | all-reduce | flops 8 | bytes 64 | tf_op jit(solution)/shard_map/pmax | solution.py:41
  464.7 5.4 %pmax.39 = f32[8]{0:T(128)} all-reduce(f32[8]{0:T(128)S(1)} %pmax.38), channel_id=1, replica_groups=mesh['row_0'=2,'row_1'=8,'row_2'=2,'feat_0'=4,'feat_1'=2] {'feat_1'}, use_global_device_ids=true, to_apply=%region_17.18 | all-reduce | flops 8 | bytes 64 | tf_op jit(solution)/shard_map/pmax | solution.py:41
  (84 shorter events, 50.3 us)
Async XLA Ops:
  9.3 12.6 %all-to-all-start = ((bf16[8,384,33]{1,2,0:T(8,128)(2,1)}), bf16[8,384,33]{1,2,0:T(8,128)(2,1)S(1)}, u32[]{:S(2)}, u32[]{:S(2)}) async-start(bf16[8,384,33]{1,2,0:T(8,128)(2,1)} %stack.2), calls=%async_computation | async-start | bytes 491520 | tf_op jit(solution)/shard_map/all_to_all | solution.py:27
  14.7 380.6 %all-reduce.3.cloned.1.call-start = ((), (), s32[]{:S(2)}) async-start(), calls=%async_computation.1 | async-start | bytes 17301504
  108.6 0.7 copy-start.1
  108.6 1.5 copy-start
  108.6 42.3 %copy-start.2 = (u32[256]{0:T(256)S(1)}, u32[256]{0:T(256)}, u32[]{:S(2)}) copy-start(u32[256]{0:T(256)} %constant.46) | copy-start | bytes 3076
Sparse Core Ops, SparseCore 0:
  108.8 286.5 all-reduce.2
